TPU v7x, 256 devices: a whole 4x4x8 slice. The times are simulated.
256 devices in a mesh: occ: 64 (over z, y, core), ao: 4 (over x).
Axes of the slice: x: 4, y: 4, z: 8, core: 2. Of those that a mesh axis runs over, the one named last changes fastest.
Arguments:
- amplitudes: bfloat16 [256, 256, 256], P('occ', None, 'ao'), may hold values from -6 to 6
- orbitals: bfloat16 [512, 256], replicated, may hold values from -0.375 to 0.375
- tiles: bfloat16 [4096, 512, 512], P('occ', None, 'ao'), may hold values from -0.125 to 0.125
- tile_count: int32 [64], replicated, may hold values from 1 to 64, 2048 in all
- tile_row: int32 [4096], replicated, may hold values from 0 to 7
- tile_src: int32 [4096, 1], replicated, may hold values from 0 to 63; in each aligned block of 64 rows (0 to 63, 64 to 127, ...) at most 2 rows name the same one
- tile_sub: int32 [4096], replicated, may hold values from 0 to 7
Outputs:
- sigma_out: bfloat16 [256, 256, 256], P('occ', None, 'ao')
Inputs may be any that keep to these rules, and one draw needn't show every extreme that they name: `tile_count`: each occ index owns between 1 and 64 live slots, the first ones of its 64 slots; some index owns exactly 64. `tile_src`: among the 64 slots of one owner no source index is named more than 2 times, and some owner names one source exactly 2 times.
All inputs are finite; a program needn't handle non-finite values.
Results may differ from a plain program's by a relative error of at most 0.024.
Values may be sent and summed in bfloat16 or wider, within the bound.
A program may use at most 128 MiB of HBM per device.

v0:
```python
import jax
import jax.numpy as jnp
from jax import lax
from jax.sharding import PartitionSpec as P


def shards(amplitudes, orbitals, tiles, tile_count, tile_row, tile_src, tile_sub):
    node_count = lax.axis_size("occ")
    own_index = lax.axis_index("occ")
    quarter = lax.axis_index("ao")
    local_occ, vir_count, vir_part = amplitudes.shape
    ao_count = orbitals.shape[0]
    ao_part = ao_count // lax.axis_size("ao")
    slot_count = tiles.shape[0]
    blocks = ao_count // node_count
    nu_rows = lax.dynamic_slice_in_dim(orbitals, quarter * ao_part, ao_part, 0)
    vir_cols = lax.dynamic_slice_in_dim(orbitals, quarter * vir_part, vir_part, 1)
    partial_x = jnp.einsum("icd,nd->icn", amplitudes, vir_cols, preferred_element_type=jnp.float32)
    half_pairs = lax.psum_scatter(
        partial_x.astype(jnp.bfloat16), "ao", scatter_dimension=2, tiled=True
    )
    pair_rows = jnp.einsum(
        "mc,icn->imn", orbitals, half_pairs, preferred_element_type=jnp.float32
    ).astype(jnp.bfloat16)
    sources = tile_src[:, 0].reshape(node_count, slot_count)
    sub_blocks = tile_sub.reshape(node_count, slot_count)
    own_src = lax.dynamic_index_in_dim(sources, own_index, 0, keepdims=False)
    home_rows = lax.all_to_all(pair_rows, "occ", split_axis=1, concat_axis=0, tiled=True)
    per_peer = max(2, (slot_count + node_count - 1) // node_count)
    matches = sources == own_index
    send_rank = jnp.cumsum(matches.astype(jnp.int32), axis=1) - 1
    levels = jnp.arange(per_peer, dtype=jnp.int32)
    chosen = matches[:, None, :] & (send_rank[:, None, :] == levels[None, :, None])
    block_id = jnp.sum(jnp.where(chosen, sub_blocks[:, None, :], 0), axis=2)
    all_occ = home_rows.shape[0]
    packed = jnp.take(home_rows, block_id.reshape(-1), axis=1).reshape(
        all_occ, node_count, per_peer, ao_part
    )
    arrived = lax.all_to_all(packed, "occ", split_axis=1, concat_axis=1, tiled=True)
    positions = jnp.arange(slot_count, dtype=jnp.int32)
    earlier = positions[:, None] > positions[None, :]
    same_src = own_src[:, None] == own_src[None, :]
    own_rank = jnp.sum((earlier & same_src).astype(jnp.int32), axis=1)
    fetched = jnp.take(
        arrived.reshape(all_occ, node_count * per_peer, ao_part),
        own_src * per_peer + own_rank,
        axis=1,
    )
    live_mask = jnp.arange(slot_count, dtype=jnp.int32) < tile_count[own_index]
    own_row = lax.dynamic_index_in_dim(
        tile_row.reshape(node_count, slot_count), own_index, 0, keepdims=False
    )
    onehot = (
        (own_row[:, None] == jnp.arange(blocks, dtype=jnp.int32)[None, :]) & live_mask[:, None]
    ).astype(jnp.bfloat16)
    products = jnp.einsum("itn,tsn->tis", fetched, tiles, preferred_element_type=jnp.float32)
    upper_part = products.astype(jnp.bfloat16)
    lower_part = (products - upper_part.astype(jnp.float32)).astype(jnp.bfloat16)
    partial_z = jnp.einsum("tr,tis->irs", onehot, upper_part, preferred_element_type=jnp.float32)
    partial_z = partial_z + jnp.einsum(
        "tr,tis->irs", onehot, lower_part, preferred_element_type=jnp.float32
    )
    ladder = lax.psum_scatter(partial_z.astype(jnp.bfloat16), "ao", scatter_dimension=2, tiled=True)
    back_rows = lax.all_to_all(ladder, "occ", split_axis=0, concat_axis=1, tiled=True)
    mixed = jnp.einsum(
        "la,ils->ias", orbitals, back_rows, preferred_element_type=jnp.float32
    ).astype(jnp.bfloat16)
    partial_s = jnp.einsum("ias,sb->iab", mixed, nu_rows, preferred_element_type=jnp.float32)
    return lax.psum_scatter(partial_s.astype(jnp.bfloat16), "ao", scatter_dimension=2, tiled=True)


def solution(mesh):
    placed = (P("occ", None, "ao"), P(), P("occ", None, "ao"), P(), P(), P(), P())
    return jax.shard_map(
        shards, mesh=mesh, in_specs=placed, out_specs=P("occ", None, "ao"), check_vma=False
    )
```

profile of v0, /device:TPU:8, one launch (start us, length us, event | category | flops | bytes accessed | tf_op | source)
XLA Modules:
  0.0 509.5 jit_solution(4199454795965634853)
XLA Ops:
  6.5 0.0 copy-start
  6.5 0.0 reduce-scatter.6.cloned.1.call-start
  6.5 0.9 copy-done
  7.5 2.4 fusion.12
  9.9 0.0 reduce-scatter.6.cloned.1.call-update
  9.9 0.5 broadcast.108
  10.4 1.4 reduce.3
  11.8 0.1 reshape_squeeze.3
  11.9 27.3 %reduce-scatter.6.cloned.1.call-done = bf16[4,256,128]{1,2,0:T(8,128)(2,1)} async-done(((bf16[4,256,512]{1,2,0:T(8,128)(2,1)}), bf16[4,256,128]{1,2,0:T(8,128)(2,1)}) %reduce-scatter.6.cloned.1.call-update) | async-done | bytes 262160 | tf_op jit(solution)/shard_map/reduce_scatter | solution.py:19
  39.1 1.3 fusion.13
  40.4 1.1 copy.41
  41.5 10.6 %all-to-all-start = ((bf16[4,512,128]{2,0,1:T(4,128)(2,1)}), bf16[4,512,128]{2,0,1:T(4,128)(2,1)S(1)}, u32[]{:S(2)}, u32[]{:S(2)}) async-start(bf16[4,512,128]{2,0,1:T(4,128)(2,1)} %copy.41), calls=%async_computation.1 | async-start | bytes 1048576 | tf_op jit(solution)/shard_map/all_to_all | solution.py:28
  52.1 0.2 reduce_window_sum.11
  52.3 0.8 broadcast_in_dim.45
  53.1 0.1 select_reduce_fusion
  53.2 0.1 copy.44
  53.3 0.1 reshape.107
  53.5 0.1 copy.39
  53.6 16.0 %all-to-all-done = bf16[4,512,128]{2,0,1:T(4,128)(2,1)S(1)} async-done(((bf16[4,512,128]{2,0,1:T(4,128)(2,1)}), bf16[4,512,128]{2,0,1:T(4,128)(2,1)S(1)}, u32[]{:S(2)}, u32[]{:S(2)}) %all-to-all-start) | async-done | bytes 524320 | tf_op jit(solution)/shard_map/all_to_all | solution.py:28
  69.6 0.1 copy.70
  69.7 0.1 copy.43
  69.8 0.1 copy.45
  69.8 6.4 %gather_fusion = bf16[128,256,128]{2,1,0:T(8,128)(2,1)} fusion(bf16[256,8,128]{2,0,1:T(8,128)(2,1)S(1)} %copy.45, s32[1024]{0:T(1024)S(1)} %pad_clamp_fusion.1), kind=kCustom, calls=%fused_computation | custom fusion | bytes 16777728 | tf_op jit(solution)/shard_map/jit(_take)/gather | solution.py:36
  76.2 7.4 %broadcast_select_fusion = bf16[256,64,2,128]{3,0,2,1:T(8,128)(2,1)} fusion(bf16[256,64,2,128]{3,0,2,1:T(8,128)(2,1)} %bitcast.74, pred[64,2]{1,0:T(8,128)(4,1)S(1)} %copy.39), kind=kLoop, calls=%fused_computation.7 | loop fusion | flops 4194304 | bytes 16777344 | tf_op jit(solution)/shard_map/jit(_take)/select_n | solution.py:36
  83.6 6.2 %all-to-all-start.1 = ((bf16[256,64,2,128]{3,0,2,1:T(8,128)(2,1)}), bf16[256,64,2,128]{3,0,2,1:T(8,128)(2,1)}, u32[]{:S(2)}, u32[]{:S(2)}) async-start(bf16[256,64,2,128]{3,0,2,1:T(8,128)(2,1)} %broadcast_select_fusion), calls=%async_computation.2 | async-start | bytes 16777216 | tf_op jit(solution)/shard_map/all_to_all | solution.py:39
  89.8 0.2 reduce-scatter.10.cloned.1.call-start
  90.0 0.0 copy-done.1
  90.1 0.1 reshape.109
  90.1 0.6 dynamic_slice.19
  90.7 0.7 iota_compare_fusion.3
  91.4 0.2 convert_reduce_fusion
  91.6 183.5 %all-to-all-done.1 = bf16[256,64,2,128]{3,0,2,1:T(8,128)(2,1)} async-done(((bf16[256,64,2,128]{3,0,2,1:T(8,128)(2,1)}), bf16[256,64,2,128]{3,0,2,1:T(8,128)(2,1)}, u32[]{:S(2)}, u32[]{:S(2)}) %all-to-all-start.1) | async-done | bytes 8388640 | tf_op jit(solution)/shard_map/all_to_all | solution.py:39
  275.1 6.5 %gather_fusion.1 = bf16[64,256,128]{2,1,0:T(8,128)(2,1)} fusion(bf16[256,128,128]{2,0,1:T(8,128)(2,1)} %bitcast.11, s32[1024]{0:T(1024)S(1)} %pad_clamp_fusion), kind=kCustom, calls=%fused_computation.1 | custom fusion | bytes 8388864 | tf_op jit(solution)/shard_map/jit(_take)/gather | solution.py:44
  281.6 19.5 %subtract_convert_fusion = (bf16[64,256,512]{2,1,0:T(8,128)(2,1)}, bf16[64,256,512]{2,1,0:T(8,128)(2,1)}) fusion(bf16[64,512,128]{2,1,0:T(8,128)(2,1)} %param.9, bf16[64,256,128]{2,1,0:T(8,128)(2,1)} %gather_fusion.1, pred[64]{0:T(512)(128)(4,1)S(1)} %compare_and_fusion.1), kind=kOutput, calls=%fused_computation.2 | convolution fusion | flops 2183135232 | bytes 46137408 | tf_op jit(solution)/shard_map/itn,tsn->tis/dot_general | solution.py:56
  301.1 16.7 %fusion = f32[256,512,8]{1,2,0:T(8,128)S(1)} fusion(bf16[64,256,512]{2,1,0:T(8,128)(2,1)} %get-tuple-element.5, s32[64]{0:T(128)S(1)} %fusion.38, pred[64]{0:T(512)(128)(4,1)S(1)} %iota_compare_fusion.3), kind=kOutput, calls=%fused_computation.3 | convolution fusion | flops 134218752 | bytes 20971840 | tf_op jit(solution)/shard_map/tr,tis->irs/dot_general | solution.py:60
  317.8 15.0 %fusion.8 = bf16[256,8,512]{2,1,0:T(8,128)(2,1)S(1)} fusion(f32[256,512,8]{1,2,0:T(8,128)S(1)} %fusion, bf16[64,256,512]{2,1,0:T(8,128)(2,1)} %get-tuple-element.6, s32[64]{0:T(128)S(1)} %fusion.38, pred[64]{0:T(512)(128)(4,1)S(1)} %iota_compare_fusion.3), kind=kOutput, calls=%fused_computation.13 | convolution fusion | flops 136315904 | bytes 23068992 | tf_op jit(solution)/shard_map/tr,tis->irs/dot_general | solution.py:59
  332.8 24.0 %copy.54 = bf16[256,8,512]{1,0,2:T(8,128)(2,1)} copy(bf16[256,8,512]{2,1,0:T(8,128)(2,1)S(1)} %fusion.8) | data formatting | bytes 4194304
  356.8 48.5 %reshape.130 = bf16[512,2048]{1,0:T(8,128)(2,1)} reshape(bf16[512,256,8]{2,1,0:T(8,128)(2,1)} %bitcast.73) | data formatting | bytes 4194304
  405.2 0.0 reduce-scatter.10.cloned.1.call-update
  405.2 28.7 %reduce-scatter.10.cloned.1.call-done = bf16[128,2048]{1,0:T(8,128)(2,1)} async-done(((bf16[512,2048]{1,0:T(8,128)(2,1)}), bf16[128,2048]{1,0:T(8,128)(2,1)}) %reduce-scatter.10.cloned.1.call-update) | async-done | bytes 524304
  434.0 11.9 %reshape.131 = bf16[128,256,8]{2,1,0:T(8,128)(2,1)} reshape(bf16[128,2048]{1,0:T(8,128)(2,1)} %reduce-scatter.10.cloned.1.call-done) | data formatting | bytes 1048576
  445.8 8.2 %copy.55 = bf16[256,8,128]{2,1,0:T(8,128)(2,1)} copy(bf16[256,8,128]{1,0,2:T(8,128)(2,1)} %bitcast.75) | data formatting | bytes 1048576
  454.0 10.5 %all-to-all-start.2 = ((bf16[256,8,128]{2,1,0:T(8,128)(2,1)}), bf16[256,8,128]{2,1,0:T(8,128)(2,1)S(1)}, u32[]{:S(2)}, u32[]{:S(2)}) async-start(bf16[256,8,128]{2,1,0:T(8,128)(2,1)} %copy.55), calls=%async_computation.3 | async-start | bytes 1048576 | tf_op jit(solution)/shard_map/all_to_all | solution.py:64
  464.6 0.0 reduce-scatter.8.cloned.1.call-start
  464.6 17.5 %all-to-all-done.2 = bf16[256,8,128]{2,1,0:T(8,128)(2,1)S(1)} async-done(((bf16[256,8,128]{2,1,0:T(8,128)(2,1)}), bf16[256,8,128]{2,1,0:T(8,128)(2,1)S(1)}, u32[]{:S(2)}, u32[]{:S(2)}) %all-to-all-start.2) | async-done | bytes 524320 | tf_op jit(solution)/shard_map/all_to_all | solution.py:64
  482.1 1.5 convolution_convert_fusion.2
  483.6 0.0 reduce-scatter.8.cloned.1.call-update
  483.6 19.4 %reduce-scatter.8.cloned.1.call-done = bf16[4,256,64]{1,2,0:T(8,128)(2,1)} async-done(((bf16[4,256,256]{1,2,0:T(8,128)(2,1)}), bf16[4,256,64]{1,2,0:T(8,128)(2,1)}) %reduce-scatter.8.cloned.1.call-update) | async-done | bytes 131088 | tf_op jit(solution)/shard_map/reduce_scatter | solution.py:69
  (13 shorter events, 0.1 us)
Async XLA Ops:
  6.5 1.0 copy-start
  6.5 32.6 %reduce-scatter.6.cloned.1.call-start = ((), (), s32[]{:S(2)}) async-start(), calls=%async_computation.6 | async-start | bytes 1310720 | tf_op jit(solution)/shard_map/reduce_scatter | solution.py:19
  41.5 28.1 %all-to-all-start = ((bf16[4,512,128]{2,0,1:T(4,128)(2,1)}), bf16[4,512,128]{2,0,1:T(4,128)(2,1)S(1)}, u32[]{:S(2)}, u32[]{:S(2)}) async-start(bf16[4,512,128]{2,0,1:T(4,128)(2,1)} %copy.41), calls=%async_computation.1 | async-start | bytes 1048576 | tf_op jit(solution)/shard_map/all_to_all | solution.py:28
  83.6 6.4 %copy-start.1 = (s32[4096]{0:T(1024)S(1)}, s32[4096]{0:T(1024)}, u32[]{:S(2)}) copy-start(s32[4096]{0:T(1024)} %param.11) | copy-start | bytes 49156
  83.6 6.5 %copy-start.2 = (s32[64]{0:T(128)S(1)}, s32[64]{0:T(128)}, u32[]{:S(2)}) copy-start(s32[64]{0:T(128)} %param.10) | copy-start | bytes 772
  83.6 191.5 %all-to-all-start.1 = ((bf16[256,64,2,128]{3,0,2,1:T(8,128)(2,1)}), bf16[256,64,2,128]{3,0,2,1:T(8,128)(2,1)}, u32[]{:S(2)}, u32[]{:S(2)}) async-start(bf16[256,64,2,128]{3,0,2,1:T(8,128)(2,1)} %broadcast_select_fusion), calls=%async_computation.2 | async-start | bytes 16777216 | tf_op jit(solution)/shard_map/all_to_all | solution.py:39
  89.8 344.1 %reduce-scatter.10.cloned.1.call-start = ((), (), s32[]{:S(2)}) async-start(), calls=%async_computation.8 | async-start | bytes 2621440
  454.0 28.1 %all-to-all-start.2 = ((bf16[256,8,128]{2,1,0:T(8,128)(2,1)}), bf16[256,8,128]{2,1,0:T(8,128)(2,1)S(1)}, u32[]{:S(2)}, u32[]{:S(2)}) async-start(bf16[256,8,128]{2,1,0:T(8,128)(2,1)} %copy.55), calls=%async_computation.3 | async-start | bytes 1048576 | tf_op jit(solution)/shard_map/all_to_all | solution.py:64
  464.6 38.4 %reduce-scatter.8.cloned.1.call-start = ((), (), s32[]{:S(2)}) async-start(), calls=%async_computation.7 | async-start | bytes 655360 | tf_op jit(solution)/shard_map/reduce_scatter | solution.py:69
Sparse Core Ops, SparseCore 0:
  10.0 29.0 reduce-scatter.5
  405.4 28.5 reduce-scatter.9
  483.8 19.2 reduce-scatter.7
where the time goes:
time: 510 us
  waiting for transfers between devices  292 us (57%)
  local copies, waits for them, and re-layouts  110 us (22%)
  matrix products  56.3 us (11%)
  starting transfers between devices  27.5 us (5%)
  between operations  13.3 us (3%)
  other arithmetic  10 us (2%)
    all_to_all x1, waiting for transfers between devices, shards(): lax.all_to_all(packed, 'occ', split_axis=1, concat_axis=1, tiled=True)  183 us
    unnamed x11, local copies, waits for them, and re-layouts  93.9 us
    unnamed x4, waiting for transfers between devices  28.8 us
    reduce_scatter x1, waiting for transfers between devices, shards(): lax.psum_scatter(partial_x.astype(jnp.bfloat16), 'ao', scatter_dimension=...  27.3 us
    dot_general x1, matrix products, shards(): jnp.einsum('itn,tsn->tis', fetched, tiles, preferred_element_type=jnp.flo...  19.5 us
    reduce_scatter x1, waiting for transfers between devices, shards(): lax.psum_scatter(partial_s.astype(jnp.bfloat16), 'ao', scatter_dimension=...  19.4 us
    all_to_all x1, waiting for transfers between devices, shards(): lax.all_to_all(ladder, 'occ', split_axis=0, concat_axis=1, tiled=True)  17.5 us
    dot_general x1, matrix products, shards(): jnp.einsum('tr,tis->irs', onehot, lower_part, preferred_element_type=jnp....  16.7 us
  transfers between devices with their start and end apart: 6, of which 6 were waited for; matrix products, arithmetic and copies ran while one was open for 1% of the time, Pallas kernels for 0%

commit v1 on v0

--- a/solution.py
+++ b/solution.py
@@ -25,7 +25,10 @@
     sources = tile_src[:, 0].reshape(node_count, slot_count)
     sub_blocks = tile_sub.reshape(node_count, slot_count)
     own_src = lax.dynamic_index_in_dim(sources, own_index, 0, keepdims=False)
-    home_rows = lax.all_to_all(pair_rows, "occ", split_axis=1, concat_axis=0, tiled=True)
+    home_rows = jnp.concatenate(
+        lax.all_to_all(jnp.stack(jnp.split(pair_rows, lax.axis_size("occ"), axis=1)), "occ", 0, 0),
+        axis=0,
+    )
     per_peer = max(2, (slot_count + node_count - 1) // node_count)
     matches = sources == own_index
     send_rank = jnp.cumsum(matches.astype(jnp.int32), axis=1) - 1

time: 510 us -> 625 us (1.23); the launches traced: 510 us -> 615 us
  local copies, waits for them, and re-layouts: 110 us -> 218 us
    another operation x0 -> x69, local copies, waits for them, and re-layouts: none -> 47.1 us  [shards(): jnp.stack(jnp.split(pair_rows, lax.axis_size('occ'), axis=1))]
    unnamed x11 -> x78, local copies, waits for them, and re-layouts: 93.9 us -> 132 us
    reshape x0 -> x2, local copies, waits for them, and re-layouts: none -> 12.3 us  [the longest x1 11.9 us: shards(): arrived.reshape(all_occ, node_count * per_peer, ao_part)]
    gather x1 -> x2, local copies, waits for them, and re-layouts: 6.39 us -> 18.3 us  [shards(): jnp.take(home_rows, block_id.reshape(-1), axis=1)]
where the time goes in v1:
time: 625 us; the launch traced here: 615 us
  waiting for transfers between devices  290 us (46%)
  local copies, waits for them, and re-layouts  218 us (35%)
  matrix products  53.9 us (9%)
  starting transfers between devices  27.8 us (4%)
  between operations  13.5 us (2%)
  other arithmetic  11.4 us (2%)
    all_to_all x1, waiting for transfers between devices, shards(): lax.all_to_all(packed, 'occ', split_axis=1, concat_axis=1, tiled=True)  181 us
    unnamed x78, local copies, waits for them, and re-layouts  132 us
    another operation x69, local copies, waits for them, and re-layouts, shards(): jnp.stack(jnp.split(pair_rows, lax.axis_size('occ'), axis=1))  47.1 us
    unnamed x4, waiting for transfers between devices  28.8 us
    reduce_scatter x1, waiting for transfers between devices, shards(): lax.psum_scatter(partial_x.astype(jnp.bfloat16), 'ao', scatter_dimension=...  26.7 us
    reduce_scatter x1, waiting for transfers between devices, shards(): lax.psum_scatter(partial_s.astype(jnp.bfloat16), 'ao', scatter_dimension=...  19.4 us
    gather x2, local copies, waits for them, and re-layouts, shards(): jnp.take(home_rows, block_id.reshape(-1), axis=1)  18.3 us
    all_to_all x1, waiting for transfers between devices, shards(): lax.all_to_all(ladder, 'occ', split_axis=0, concat_axis=1, tiled=True)  17.5 us
  transfers between devices with their start and end apart: 6, of which 6 were waited for; matrix products, arithmetic and copies ran while one was open for 1% of the time, Pallas kernels for 0%

profile of v1, /device:TPU:8, one launch (start us, length us, event | category | flops | bytes accessed | tf_op | source)
XLA Modules:
  0.0 614.9 jit_solution(16077765263909051606)
XLA Ops:
  7.5 2.4 fusion.12
  10.4 1.4 reduce.3
  12.5 26.7 %reduce-scatter.6.cloned.1.call-done = bf16[4,256,128]{1,2,0:T(8,128)(2,1)} async-done(((bf16[4,256,512]{1,2,0:T(8,128)(2,1)}), bf16[4,256,128]{1,2,0:T(8,128)(2,1)}) %reduce-scatter.6.cloned.1.call-update) | async-done | bytes 262160 | tf_op jit(solution)/shard_map/reduce_scatter | solution.py:19
  39.1 1.3 fusion.13
  40.7 2.1 slice_bitcast_fusion.38
  42.8 2.2 slice_bitcast_fusion.19
  45.0 1.3 slice_bitcast_fusion
  47.5 1.0 copy.177
  48.5 1.0 copy.178
  49.5 1.0 copy.179
  50.5 1.0 copy.180
  51.5 1.0 copy.181
  52.4 1.0 copy.182
  53.4 1.0 copy.183
  54.4 1.0 copy.184
  55.4 1.0 copy.185
  56.4 1.0 copy.186
  57.4 1.0 copy.187
  58.3 1.0 copy.188
  59.3 1.0 copy.189
  60.3 1.0 copy.190
  61.3 1.0 copy.191
  62.3 1.0 copy.192
  72.1 1.0 copy.202
  74.1 1.0 copy.204
  76.1 1.0 copy.206
  78.0 1.0 copy.208
  125.1 10.6 %all-to-all-start = ((bf16[64,4,8,128]{3,2,1,0:T(8,128)(2,1)}), bf16[64,4,8,128]{3,2,1,0:T(8,128)(2,1)S(1)}, u32[]{:S(2)}, u32[]{:S(2)}) async-start(bf16[64,4,8,128]{3,2,1,0:T(8,128)(2,1)} %constant_dynamic-update-slice_fusion), calls=%async_computation.1 | async-start | bytes 1048576 | tf_op jit(solution)/shard_map/all_to_all | solution.py:29
  136.5 16.7 %all-to-all-done = bf16[64,4,8,128]{3,2,1,0:T(8,128)(2,1)S(1)} async-done(((bf16[64,4,8,128]{3,2,1,0:T(8,128)(2,1)}), bf16[64,4,8,128]{3,2,1,0:T(8,128)(2,1)S(1)}, u32[]{:S(2)}, u32[]{:S(2)}) %all-to-all-start) | async-done | bytes 524320 | tf_op jit(solution)/shard_map/all_to_all | solution.py:29
  153.5 6.4 %gather_fusion = bf16[128,256,128]{1,2,0:T(8,128)(2,1)} fusion(bf16[256,8,128]{0,2,1:T(8,128)(2,1)S(1)} %copy.235, s32[1024]{0:T(1024)S(1)} %pad_clamp_fusion.1), kind=kCustom, calls=%fused_computation | custom fusion | bytes 16777728 | tf_op jit(solution)/shard_map/jit(_take)/gather | solution.py:39
  159.9 12.0 %copy.236 = bf16[256,128,128]{2,0,1:T(8,128)(2,1)} copy(bf16[256,128,128]{0,2,1:T(8,128)(2,1)} %bitcast.196) | data formatting | bytes 16777216 | tf_op jit(solution)/shard_map/jit(_take)/gather | solution.py:39
  171.9 7.4 %broadcast_select_fusion = bf16[256,64,2,128]{3,0,2,1:T(8,128)(2,1)} fusion(bf16[256,64,2,128]{3,0,2,1:T(8,128)(2,1)} %bitcast.197, pred[64,2]{1,0:T(8,128)(4,1)S(1)} %copy.168), kind=kLoop, calls=%fused_computation.7 | loop fusion | flops 4194304 | bytes 16777344 | tf_op jit(solution)/shard_map/jit(_take)/select_n | solution.py:39
  179.3 6.2 %all-to-all-start.1 = ((bf16[256,64,2,128]{3,0,2,1:T(8,128)(2,1)}), bf16[256,64,2,128]{3,0,2,1:T(8,128)(2,1)}, u32[]{:S(2)}, u32[]{:S(2)}) async-start(bf16[256,64,2,128]{3,0,2,1:T(8,128)(2,1)} %broadcast_select_fusion), calls=%async_computation.2 | async-start | bytes 16777216 | tf_op jit(solution)/shard_map/all_to_all | solution.py:42
  189.6 181.2 %all-to-all-done.1 = bf16[256,64,2,128]{3,0,2,1:T(8,128)(2,1)} async-done(((bf16[256,64,2,128]{3,0,2,1:T(8,128)(2,1)}), bf16[256,64,2,128]{3,0,2,1:T(8,128)(2,1)}, u32[]{:S(2)}, u32[]{:S(2)}) %all-to-all-start.1) | async-done | bytes 8388640 | tf_op jit(solution)/shard_map/all_to_all | solution.py:42
  370.7 11.9 %copy.237 = bf16[256,128,128]{0,2,1:T(8,128)(2,1)} copy(bf16[256,128,128]{2,0,1:T(8,128)(2,1)} %bitcast.73) | data formatting | bytes 16777216 | tf_op jit(solution)/shard_map/reshape | solution.py:48
  382.7 6.2 %gather_fusion.1 = bf16[64,256,128]{1,2,0:T(8,128)(2,1)} fusion(bf16[256,128,128]{0,2,1:T(8,128)(2,1)} %copy.237, s32[1024]{0:T(1024)S(1)} %pad_clamp_fusion), kind=kCustom, calls=%fused_computation.1 | custom fusion | bytes 8388864 | tf_op jit(solution)/shard_map/jit(_take)/gather | solution.py:47
  388.9 17.0 %subtract_convert_fusion = (bf16[64,256,512]{2,1,0:T(8,128)(2,1)}, bf16[64,256,512]{2,1,0:T(8,128)(2,1)}) fusion(bf16[64,512,128]{2,1,0:T(8,128)(2,1)} %param.9, bf16[64,256,128]{1,2,0:T(8,128)(2,1)} %gather_fusion.1, pred[64]{0:T(512)(128)(4,1)S(1)} %compare_and_fusion.1), kind=kOutput, calls=%fused_computation.2 | convolution fusion | flops 2183135232 | bytes 46137408 | tf_op jit(solution)/shard_map/itn,tsn->tis/dot_general | solution.py:59
  406.0 16.7 %fusion = f32[256,512,8]{1,2,0:T(8,128)S(1)} fusion(bf16[64,256,512]{2,1,0:T(8,128)(2,1)} %get-tuple-element.5, s32[64]{0:T(128)S(1)} %fusion.38, pred[64]{0:T(512)(128)(4,1)S(1)} %iota_compare_fusion.3), kind=kOutput, calls=%fused_computation.3 | convolution fusion | flops 134218752 | bytes 20971840 | tf_op jit(solution)/shard_map/tr,tis->irs/dot_general | solution.py:63
  422.7 15.0 %fusion.8 = bf16[256,8,512]{2,1,0:T(8,128)(2,1)S(1)} fusion(f32[256,512,8]{1,2,0:T(8,128)S(1)} %fusion, bf16[64,256,512]{2,1,0:T(8,128)(2,1)} %get-tuple-element.6, s32[64]{0:T(128)S(1)} %fusion.38, pred[64]{0:T(512)(128)(4,1)S(1)} %iota_compare_fusion.3), kind=kOutput, calls=%fused_computation.13 | convolution fusion | flops 136315904 | bytes 23068992 | tf_op jit(solution)/shard_map/tr,tis->irs/dot_general | solution.py:62
  437.7 23.9 %copy.248 = bf16[256,8,512]{1,0,2:T(8,128)(2,1)} copy(bf16[256,8,512]{2,1,0:T(8,128)(2,1)S(1)} %fusion.8) | data formatting | bytes 4194304
  461.6 48.5 %reshape.134 = bf16[512,2048]{1,0:T(8,128)(2,1)} reshape(bf16[512,256,8]{2,1,0:T(8,128)(2,1)} %bitcast.195) | data formatting | bytes 4194304
  510.1 28.7 %reduce-scatter.10.cloned.1.call-done = bf16[128,2048]{1,0:T(8,128)(2,1)} async-done(((bf16[512,2048]{1,0:T(8,128)(2,1)}), bf16[128,2048]{1,0:T(8,128)(2,1)}) %reduce-scatter.10.cloned.1.call-update) | async-done | bytes 524304
  538.8 12.1 %reshape.135 = bf16[128,256,8]{2,1,0:T(8,128)(2,1)} reshape(bf16[128,2048]{1,0:T(8,128)(2,1)} %reduce-scatter.10.cloned.1.call-done) | data formatting | bytes 1048576
  550.9 8.2 %copy.249 = bf16[256,8,128]{2,1,0:T(8,128)(2,1)} copy(bf16[256,8,128]{1,0,2:T(8,128)(2,1)} %bitcast.198) | data formatting | bytes 1048576
  559.1 10.6 %all-to-all-start.2 = ((bf16[256,8,128]{2,1,0:T(8,128)(2,1)}), bf16[256,8,128]{2,1,0:T(8,128)(2,1)S(1)}, u32[]{:S(2)}, u32[]{:S(2)}) async-start(bf16[256,8,128]{2,1,0:T(8,128)(2,1)} %copy.249), calls=%async_computation.3 | async-start | bytes 1048576 | tf_op jit(solution)/shard_map/all_to_all | solution.py:67
  569.7 17.5 %all-to-all-done.2 = bf16[256,8,128]{2,1,0:T(8,128)(2,1)S(1)} async-done(((bf16[256,8,128]{2,1,0:T(8,128)(2,1)}), bf16[256,8,128]{2,1,0:T(8,128)(2,1)S(1)}, u32[]{:S(2)}, u32[]{:S(2)}) %all-to-all-start.2) | async-done | bytes 524320 | tf_op jit(solution)/shard_map/all_to_all | solution.py:67
  587.2 1.5 convolution_convert_fusion.2
  588.8 19.4 %reduce-scatter.8.cloned.1.call-done = bf16[4,256,64]{1,2,0:T(8,128)(2,1)} async-done(((bf16[4,256,256]{1,2,0:T(8,128)(2,1)}), bf16[4,256,64]{1,2,0:T(8,128)(2,1)}) %reduce-scatter.8.cloned.1.call-update) | async-done | bytes 131088 | tf_op jit(solution)/shard_map/reduce_scatter | solution.py:72
  (148 shorter events, 66.8 us)
Async XLA Ops:
  6.5 1.0 copy-start
  6.5 32.6 %reduce-scatter.6.cloned.1.call-start = ((), (), s32[]{:S(2)}) async-start(), calls=%async_computation.6 | async-start | bytes 1310720 | tf_op jit(solution)/shard_map/reduce_scatter | solution.py:19
  47.0 88.9 %copy-start.2 = (s32[4096]{0:T(1024)S(1)}, s32[4096]{0:T(1024)}, u32[]{:S(2)}) copy-start(s32[4096]{0:T(1024)} %param.13) | copy-start | bytes 49156
  47.2 88.4 %copy-start.1 = (s32[64,64]{1,0:T(8,128)S(1)}, s32[64,64]{1,0:T(8,128)}, u32[]{:S(2)}) copy-start(s32[64,64]{1,0:T(8,128)} %reshape_squeeze.3) | copy-start | bytes 49156
  125.1 28.1 %all-to-all-start = ((bf16[64,4,8,128]{3,2,1,0:T(8,128)(2,1)}), bf16[64,4,8,128]{3,2,1,0:T(8,128)(2,1)S(1)}, u32[]{:S(2)}, u32[]{:S(2)}) async-start(bf16[64,4,8,128]{3,2,1,0:T(8,128)(2,1)} %constant_dynamic-update-slice_fusion), calls=%async_computation.1 | async-start | bytes 1048576 | tf_op jit(solution)/shard_map/all_to_all | solution.py:29
  179.3 6.7 %copy-start.3 = (s32[4096]{0:T(1024)S(1)}, s32[4096]{0:T(1024)}, u32[]{:S(2)}) copy-start(s32[4096]{0:T(1024)} %param.11) | copy-start | bytes 49156
  179.3 6.8 %copy-start.4 = (s32[64]{0:T(128)S(1)}, s32[64]{0:T(128)}, u32[]{:S(2)}) copy-start(s32[64]{0:T(128)} %param.10) | copy-start | bytes 772
  179.3 191.5 %all-to-all-start.1 = ((bf16[256,64,2,128]{3,0,2,1:T(8,128)(2,1)}), bf16[256,64,2,128]{3,0,2,1:T(8,128)(2,1)}, u32[]{:S(2)}, u32[]{:S(2)}) async-start(bf16[256,64,2,128]{3,0,2,1:T(8,128)(2,1)} %broadcast_select_fusion), calls=%async_computation.2 | async-start | bytes 16777216 | tf_op jit(solution)/shard_map/all_to_all | solution.py:42
  185.5 353.4 %reduce-scatter.10.cloned.1.call-start = ((), (), s32[]{:S(2)}) async-start(), calls=%async_computation.8 | async-start | bytes 2621440
  559.1 28.1 %all-to-all-start.2 = ((bf16[256,8,128]{2,1,0:T(8,128)(2,1)}), bf16[256,8,128]{2,1,0:T(8,128)(2,1)S(1)}, u32[]{:S(2)}, u32[]{:S(2)}) async-start(bf16[256,8,128]{2,1,0:T(8,128)(2,1)} %copy.249), calls=%async_computation.3 | async-start | bytes 1048576 | tf_op jit(solution)/shard_map/all_to_all | solution.py:67
  569.7 38.4 %reduce-scatter.8.cloned.1.call-start = ((), (), s32[]{:S(2)}) async-start(), calls=%async_computation.7 | async-start | bytes 655360 | tf_op jit(solution)/shard_map/reduce_scatter | solution.py:72
Sparse Core Ops, SparseCore 0:
  10.0 29.0 reduce-scatter.5
  510.2 28.5 reduce-scatter.9
  588.9 19.2 reduce-scatter.7
